TPU v7x, 32 devices: a whole 2x2x4 slice. The times are simulated.
32 devices in a mesh: seq: 4 (over y, core), head: 8 (over z, x).
Axes of the slice: x: 2, y: 2, z: 4, core: 2. Of those that a mesh axis runs over, the one named last changes fastest.
Arguments:
- query_rows: bfloat16 [4096, 8192], P(('seq', 'head')), may hold values from -6 to 6
- key_rows: bfloat16 [4096, 1024], P(('seq', 'head')), may hold values from -6 to 6
- value_rows: bfloat16 [4096, 1024], P(('seq', 'head')), may hold values from -6 to 6
- grad_out: bfloat16 [8192, 8192], P(('seq', 'head')), may hold values from -6 to 6
- doc_ids: int32 [32], replicated, may hold values from 0 to 7, never falling along the last dimension, each value on 1 to 7 neighbouring positions
- route_table: int32 [4, 4, 4], replicated, may hold values from 0 to 8, as said below
Outputs:
- attn_out: bfloat16 [8192, 8192], P(('seq', 'head'))
- grad_query: bfloat16 [4096, 8192], P(('seq', 'head'))
- grad_key: bfloat16 [4096, 1024], P(('seq', 'head'))
- grad_value: bfloat16 [4096, 1024], P(('seq', 'head'))
Inputs may be any that keep to these rules, and one draw needn't show every extreme that they name: route_table[s, t, c] is a block of sequence shard s (numbered within the shard) that seq index t takes into slot c, or 8 for an empty slot; every block of every shard appears exactly once; live slots come first in each (s, t) row; each shard fills all 4 slots for a quarter of the seq indices, 2 slots for half of them and none for the rest; one seq index has every slot live.
All inputs are finite; a program needn't handle non-finite values.
Results may differ from a plain program's by a relative error of at most 0.015.
Values may be sent and summed in bfloat16 or wider, within the bound.
No kernel may reach another device: no remote copies, remote signals or barrier semaphores. Data moves between devices by JAX's collectives and lax.ppermute only.
A program may use at most 192 MiB of HBM per device.

v0:
```python
import math
import jax
import jax.numpy as jnp
from jax import lax
from jax.sharding import PartitionSpec as P

QH = 64
KVH = 8
DH = 128
BLOCK = 128
DOCMAX = 7


def slot_pass(queries, cotangent, keys_win, values_win, allowed, alive_flag, factor):
    scores = (
        jnp.einsum("bpd,nd->pbn", queries, keys_win, preferred_element_type=jnp.float32) * factor
    )
    scores = jnp.where(allowed[None], scores, -jnp.inf)
    rowmax = jnp.max(scores, axis=-1, keepdims=True)
    exponent = jnp.where(allowed[None], jnp.exp(scores - rowmax), jnp.zeros_like(scores))
    weights = exponent / jnp.sum(exponent, axis=-1, keepdims=True)
    weights_b = weights.astype(jnp.bfloat16)
    output = jnp.einsum("pbn,nd->bpd", weights_b, values_win, preferred_element_type=jnp.float32)
    output = jnp.where(alive_flag, output, jnp.zeros_like(output)).astype(jnp.bfloat16)
    cotangent = jnp.where(alive_flag, cotangent, jnp.zeros_like(cotangent))
    deltas = jnp.sum(cotangent.astype(jnp.float32) * output.astype(jnp.float32), axis=-1)
    prob_grad = jnp.einsum("bpd,nd->pbn", cotangent, values_win, preferred_element_type=jnp.float32)
    dscore = (weights * (prob_grad - deltas.T[:, :, None]) * factor).astype(jnp.bfloat16)
    grad_rows = jnp.einsum(
        "pbn,nd->bpd", dscore, keys_win, preferred_element_type=jnp.float32
    ).astype(jnp.bfloat16)
    key_part = jnp.einsum("pbn,bpd->nd", dscore, queries, preferred_element_type=jnp.float32)
    value_part = jnp.einsum("pbn,bpd->nd", weights_b, cotangent, preferred_element_type=jnp.float32)
    return (output, grad_rows, jnp.concatenate([key_part, value_part], axis=-1))


def body(query_rows, key_rows, value_rows, grad_out, doc_ids, route_table):
    tok_count = query_rows.shape[0]
    heads_axis = lax.axis_size("head")
    seq_count = lax.axis_size("seq")
    per_dev = QH // heads_axis
    repeats = heads_axis // KVH
    blocks_shard = tok_count * heads_axis // BLOCK
    slot_cap = route_table.shape[2]
    slot_total = seq_count * slot_cap
    total_tok = tok_count * heads_axis * seq_count
    window = DOCMAX * BLOCK
    margin = (DOCMAX - 1) * BLOCK
    factor = 1.0 / math.sqrt(DH)
    query_split = query_rows.reshape(tok_count, heads_axis, per_dev * DH)
    key_value = jnp.concatenate(
        [key_rows.reshape(tok_count, KVH, 1, DH), value_rows.reshape(tok_count, KVH, 1, DH)],
        axis=-1,
    )
    key_value = jnp.broadcast_to(key_value, (tok_count, KVH, repeats, 2 * DH)).reshape(
        tok_count, heads_axis, 2 * DH
    )
    query_local, pairs_local = (
        lax.all_to_all(query_split, "head", split_axis=1, concat_axis=0, tiled=True),
        lax.all_to_all(key_value, "head", split_axis=1, concat_axis=0, tiled=True),
    )
    pairs_all = lax.all_gather(pairs_local, "seq", axis=0, tiled=True).reshape(total_tok, 2 * DH)
    grad_split = grad_out.reshape(2 * tok_count, heads_axis, per_dev * DH)
    grad_local = lax.all_to_all(
        grad_split, "head", split_axis=1, concat_axis=0, tiled=True
    ).reshape(slot_total, BLOCK, per_dev, DH)
    seq_self = lax.axis_index("seq")
    send_index = lax.dynamic_index_in_dim(route_table, seq_self, 0, keepdims=False)
    send_live = send_index < blocks_shard
    send_safe = jnp.where(send_live, send_index, 0)
    query_blocks = query_local.reshape(blocks_shard, BLOCK, per_dev * DH)
    outgoing = jnp.take(query_blocks, send_safe.reshape(-1), axis=0).reshape(
        seq_count, slot_cap, BLOCK, per_dev * DH
    )
    incoming = lax.all_to_all(outgoing, "seq", split_axis=0, concat_axis=0, tiled=True).reshape(
        slot_total, BLOCK, per_dev, DH
    )
    recv_index = lax.dynamic_index_in_dim(route_table, seq_self, 1, keepdims=False).reshape(-1)
    alive_slot = recv_index < blocks_shard
    source = jnp.repeat(jnp.arange(seq_count, dtype=jnp.int32), slot_cap)
    block_ids = jnp.where(alive_slot, source * blocks_shard + recv_index, 0)
    pairs_pad = jnp.concatenate([jnp.zeros((margin, 2 * DH), jnp.bfloat16), pairs_all], axis=0)
    doc_pad = jnp.concatenate([jnp.full((DOCMAX - 1,), -1, jnp.int32), doc_ids])
    columns = jnp.arange(window)
    row_pos = jnp.arange(BLOCK)
    causal = (columns[None, :] < margin) | (columns[None, :] - margin <= row_pos[:, None])
    group_size = 4
    group_count = slot_total // group_size

    def one_slot(queries, cotangent, block_id, alive_flag):
        pairs_win = lax.dynamic_slice_in_dim(pairs_pad, block_id * BLOCK, window, 0)
        docs_win = lax.dynamic_slice_in_dim(doc_pad, block_id, DOCMAX, 0)
        same_doc = jnp.repeat(docs_win == docs_win[DOCMAX - 1], BLOCK)
        allowed = causal & same_doc[None, :]
        return slot_pass(
            queries, cotangent, pairs_win[:, :DH], pairs_win[:, DH:], allowed, alive_flag, factor
        )

    def group_step(partial_value, group_index):
        first_slot = group_index * group_size
        queries = lax.dynamic_slice_in_dim(incoming, first_slot, group_size, 0)
        cotangent = lax.dynamic_slice_in_dim(grad_local, first_slot, group_size, 0)
        slot_ids = lax.dynamic_slice_in_dim(block_ids, first_slot, group_size, 0)
        alive_flags = lax.dynamic_slice_in_dim(alive_slot, first_slot, group_size, 0)
        outputs, grad_rows, updates = jax.vmap(one_slot)(queries, cotangent, slot_ids, alive_flags)
        for member in range(group_size):
            row_start = slot_ids[member] * BLOCK
            current = lax.dynamic_slice_in_dim(partial_value, row_start, window, 0)
            partial_value = lax.dynamic_update_slice_in_dim(
                partial_value, current + updates[member], row_start, 0
            )
        return (partial_value, (outputs, grad_rows))

    partial_init = jnp.zeros((margin + total_tok, 2 * DH), jnp.float32)
    partial_value, (outputs, grad_rows) = lax.scan(
        group_step, partial_init, jnp.arange(group_count)
    )
    out_slots = outputs.reshape(slot_total * BLOCK, 1, per_dev * DH)
    attn_out = lax.all_to_all(out_slots, "head", split_axis=0, concat_axis=1, tiled=True).reshape(
        2 * tok_count, QH * DH
    )
    back_slots = grad_rows.reshape(seq_count, slot_cap, BLOCK, per_dev * DH)
    returned = lax.all_to_all(back_slots, "seq", split_axis=0, concat_axis=0, tiled=True).reshape(
        slot_total, BLOCK, per_dev * DH
    )
    place_idx = jnp.where(send_live, send_index, blocks_shard).reshape(-1)
    own_blocks = (
        jnp.zeros((blocks_shard + 1, BLOCK, per_dev * DH), jnp.bfloat16).at[place_idx].set(returned)
    )
    own_rows = own_blocks[:blocks_shard].reshape(blocks_shard * BLOCK, 1, per_dev * DH)
    grad_query = lax.all_to_all(own_rows, "head", split_axis=0, concat_axis=1, tiled=True).reshape(
        tok_count, QH * DH
    )
    summed_rows = lax.psum_scatter(
        partial_value[margin:].astype(jnp.bfloat16), "seq", scatter_dimension=0, tiled=True
    )
    summed_rows = summed_rows.reshape(blocks_shard * BLOCK, 1, 2 * DH)
    spread = lax.all_to_all(summed_rows, "head", split_axis=0, concat_axis=1, tiled=True)
    merged = jnp.sum(
        spread.reshape(tok_count, KVH, repeats, 2 * DH).astype(jnp.float32), axis=2
    ).astype(jnp.bfloat16)
    grad_key = merged[:, :, :DH].reshape(tok_count, KVH * DH)
    grad_value = merged[:, :, DH:].reshape(tok_count, KVH * DH)
    return (attn_out, grad_query, grad_key, grad_value)


def solution(mesh):
    in_specs = (
        P(("seq", "head"), None),
        P(("seq", "head"), None),
        P(("seq", "head"), None),
        P(("seq", "head"), None),
        P(),
        P(),
    )
    out_specs = (
        P(("seq", "head"), None),
        P(("seq", "head"), None),
        P(("seq", "head"), None),
        P(("seq", "head"), None),
    )
    return jax.shard_map(body, mesh=mesh, in_specs=in_specs, out_specs=out_specs, check_vma=False)
```

profile of v0, /device:TPU:0, one launch (start us, length us, event | category | flops | bytes accessed | tf_op | source)
XLA Modules:
  0.0 827.7 jit_solution(8605407508596196306)
XLA Ops:
  10.1 7.3 all-to-all-start
  23.2 8.7 %all-to-all-done = bf16[128,8,256]{2,0,1:T(8,128)(2,1)S(1)} async-done(((bf16[128,8,256]{2,0,1:T(8,128)(2,1)}), bf16[128,8,256]{2,0,1:T(8,128)(2,1)S(1)}, u32[]{:S(2)}, u32[]{:S(2)}) %all-to-all-start) | async-done | bytes 524320 | tf_op jit(solution)/shard_map/all_to_all | solution.py:60
  40.3 43.6 %all-to-all-done.1 = bf16[128,8,1024]{2,0,1:T(8,128)(2,1)S(1)} async-done(((bf16[128,8,1024]{2,0,1:T(8,128)(2,1)}), bf16[128,8,1024]{2,0,1:T(8,128)(2,1)S(1)}, u32[]{:S(2)}, u32[]{:S(2)}) %all-to-all-start.1) | async-done | bytes 2097184 | tf_op jit(solution)/shard_map/all_to_all | solution.py:59
  103.4 77.7 %all-to-all-done.3 = bf16[256,8,1024]{2,0,1:T(8,128)(2,1)} async-done(((bf16[256,8,1024]{2,0,1:T(8,128)(2,1)}), bf16[256,8,1024]{2,0,1:T(8,128)(2,1)}, u32[]{:S(2)}, u32[]{:S(2)}) %all-to-all-start.3) | async-done | bytes 4194336 | tf_op jit(solution)/shard_map/all_to_all | solution.py:64
  194.9 39.3 %all-to-all-done.2 = bf16[4,4,128,1024]{2,3,1,0:T(8,128)(2,1)} async-done(((bf16[4,4,128,1024]{2,3,1,0:T(8,128)(2,1)}), bf16[4,4,128,1024]{2,3,1,0:T(8,128)(2,1)}, u32[]{:S(2)}, u32[]{:S(2)}) %all-to-all-start.2) | async-done | bytes 4194336 | tf_op jit(solution)/shard_map/all_to_all | solution.py:75
  236.8 298.6 %while.23 = (s32[]{:T(128)}, f32[4864,256]{0,1:T(8,128)}, bf16[4,4,128,8,128]{4,3,2,1,0:T(8,128)(2,1)}, bf16[4,4,128,8,128]{2,4,3,1,0:T(8,128)(2,1)}, s32[4]{0:T...) while((s32[]{:T(128)}, f32[4864,256]{0,1:T(8,128)}, ...), condition=%wide.region_4.5_spmd.clone, body=%wide.region_0.0_spmd.clone.sunk | while | flops 5688947712 | bytes 244061568 | solution.py:115
  250.2 9.5 %while.25 = (s32[]{:T(128)}, bf16[4864,256]{1,0:T(8,128)(2,1)}, s32[4,2]{0,1:T(2,128)S(1)}, bf16[4,896,256]{2,1,0:T(8,128)(2,1)S(1)}, s32[]{:T(128)}) while((s32[]{:T(128)}, bf16[4864,256]{1,0:T(8,128)(2,1)}, s32[4,2]{0,1:T(2,128)S(1)}, bf16[4,896,256]{2,1,0:T(8,128)(2,1)S(1)}, s32[]{:T(128)}) %tuple.86), condition=%wide.while_cond.1, body=%wide.while_body.1.sunk | while | flops 2 | bytes 917609 | solution.py:91
  259.8 10.0 %fusion.113 = (f32[4,8,128]{2,1,0:T(8,128)S(1)}, f32[4,8,128,896]{2,3,1,0:T(8,128)}) fusion(pred[4,128,896]{1,2,0:T(8,128)(4,1)S(1)} %broadcast_and_fusion.2, bf16[16,128,8,128]{1,3,2,0:T(8,128)(2,1)} %get-tuple-element.513, s32[]{:T(128)S(6)} %select_n.197, bf16[4,896,256]{2,1,0:T(8,128)(2,1)S(1)} %get-tuple-element.411), kind=kOutput, calls=%fused_computation.105.clone.1 | convolution fusion | flops 957875072 | bytes 17580036 | tf_op jit(solution)/shard_map/while/body/eval_jaxpr/vmap()/sub | solution.py:20
  269.8 9.9 %fusion.114 = bf16[4,8,128,896]{2,3,1,0:T(8,128)(2,1)} fusion(f32[4,8,128,896]{2,3,1,0:T(8,128)} %get-tuple-element.412, f32[4,8,128]{2,1,0:T(8,128)S(1)} %get-tuple-element.413), kind=kLoop, calls=%fused_computation.19.clone.1 | loop fusion | flops 7340032 | bytes 22036480 | tf_op jit(solution)/shard_map/while/body/eval_jaxpr/vmap()/convert_element_type | solution.py:22
  287.7 8.5 %fusion.115 = bf16[4,8,128,896]{2,3,1,0:T(8,128)(2,1)} fusion(f32[4,8,128]{2,1,0:T(8,128)S(1)} %bitcast.276, f32[4,8,128,896]{2,3,1,0:T(8,128)} %get-tuple-element.412, f32[4,8,128]{2,1,0:T(8,128)S(1)} %get-tuple-element.413, bf16[4,896,256]{2,1,0:T(8,128)(2,1)S(1)} %copy-done.4, bf16[4,128,8,128]{1,3,2,0:T(8,128)(2,1)S(1)} %copy.188, ...), kind=kOutput, calls=%fused_computation.11.clone.1 | convolution fusion | flops 958398464 | bytes 24019456 | tf_op jit(solution)/shard_map/while/body/eval_jaxpr/vmap(bpd,nd->pbn)/dot_general | solution.py:27
  324.9 9.5 %while.25 = (s32[]{:T(128)}, bf16[4864,256]{1,0:T(8,128)(2,1)}, s32[4,2]{0,1:T(2,128)S(1)}, bf16[4,896,256]{2,1,0:T(8,128)(2,1)S(1)}, s32[]{:T(128)}) while((s32[]{:T(128)}, bf16[4864,256]{1,0:T(8,128)(2,1)}, s32[4,2]{0,1:T(2,128)S(1)}, bf16[4,896,256]{2,1,0:T(8,128)(2,1)S(1)}, s32[]{:T(128)}) %tuple.86), condition=%wide.while_cond.1, body=%wide.while_body.1.sunk | while | flops 2 | bytes 917609 | solution.py:91
  334.5 10.0 %fusion.113 = (f32[4,8,128]{2,1,0:T(8,128)S(1)}, f32[4,8,128,896]{2,3,1,0:T(8,128)}) fusion(pred[4,128,896]{1,2,0:T(8,128)(4,1)S(1)} %broadcast_and_fusion.2, bf16[16,128,8,128]{1,3,2,0:T(8,128)(2,1)} %get-tuple-element.513, s32[]{:T(128)S(6)} %select_n.197, bf16[4,896,256]{2,1,0:T(8,128)(2,1)S(1)} %get-tuple-element.411), kind=kOutput, calls=%fused_computation.105.clone.1 | convolution fusion | flops 957875072 | bytes 17580036 | tf_op jit(solution)/shard_map/while/body/eval_jaxpr/vmap()/sub | solution.py:20
  344.4 9.9 %fusion.114 = bf16[4,8,128,896]{2,3,1,0:T(8,128)(2,1)} fusion(f32[4,8,128,896]{2,3,1,0:T(8,128)} %get-tuple-element.412, f32[4,8,128]{2,1,0:T(8,128)S(1)} %get-tuple-element.413), kind=kLoop, calls=%fused_computation.19.clone.1 | loop fusion | flops 7340032 | bytes 22036480 | tf_op jit(solution)/shard_map/while/body/eval_jaxpr/vmap()/convert_element_type | solution.py:22
  362.4 8.5 %fusion.115 = bf16[4,8,128,896]{2,3,1,0:T(8,128)(2,1)} fusion(f32[4,8,128]{2,1,0:T(8,128)S(1)} %bitcast.276, f32[4,8,128,896]{2,3,1,0:T(8,128)} %get-tuple-element.412, f32[4,8,128]{2,1,0:T(8,128)S(1)} %get-tuple-element.413, bf16[4,896,256]{2,1,0:T(8,128)(2,1)S(1)} %copy-done.4, bf16[4,128,8,128]{1,3,2,0:T(8,128)(2,1)S(1)} %copy.188, ...), kind=kOutput, calls=%fused_computation.11.clone.1 | convolution fusion | flops 958398464 | bytes 24019456 | tf_op jit(solution)/shard_map/while/body/eval_jaxpr/vmap(bpd,nd->pbn)/dot_general | solution.py:27
  399.6 9.5 %while.25 = (s32[]{:T(128)}, bf16[4864,256]{1,0:T(8,128)(2,1)}, s32[4,2]{0,1:T(2,128)S(1)}, bf16[4,896,256]{2,1,0:T(8,128)(2,1)S(1)}, s32[]{:T(128)}) while((s32[]{:T(128)}, bf16[4864,256]{1,0:T(8,128)(2,1)}, s32[4,2]{0,1:T(2,128)S(1)}, bf16[4,896,256]{2,1,0:T(8,128)(2,1)S(1)}, s32[]{:T(128)}) %tuple.86), condition=%wide.while_cond.1, body=%wide.while_body.1.sunk | while | flops 2 | bytes 917609 | solution.py:91
  409.2 10.0 %fusion.113 = (f32[4,8,128]{2,1,0:T(8,128)S(1)}, f32[4,8,128,896]{2,3,1,0:T(8,128)}) fusion(pred[4,128,896]{1,2,0:T(8,128)(4,1)S(1)} %broadcast_and_fusion.2, bf16[16,128,8,128]{1,3,2,0:T(8,128)(2,1)} %get-tuple-element.513, s32[]{:T(128)S(6)} %select_n.197, bf16[4,896,256]{2,1,0:T(8,128)(2,1)S(1)} %get-tuple-element.411), kind=kOutput, calls=%fused_computation.105.clone.1 | convolution fusion | flops 957875072 | bytes 17580036 | tf_op jit(solution)/shard_map/while/body/eval_jaxpr/vmap()/sub | solution.py:20
  419.1 9.9 %fusion.114 = bf16[4,8,128,896]{2,3,1,0:T(8,128)(2,1)} fusion(f32[4,8,128,896]{2,3,1,0:T(8,128)} %get-tuple-element.412, f32[4,8,128]{2,1,0:T(8,128)S(1)} %get-tuple-element.413), kind=kLoop, calls=%fused_computation.19.clone.1 | loop fusion | flops 7340032 | bytes 22036480 | tf_op jit(solution)/shard_map/while/body/eval_jaxpr/vmap()/convert_element_type | solution.py:22
  437.1 8.5 %fusion.115 = bf16[4,8,128,896]{2,3,1,0:T(8,128)(2,1)} fusion(f32[4,8,128]{2,1,0:T(8,128)S(1)} %bitcast.276, f32[4,8,128,896]{2,3,1,0:T(8,128)} %get-tuple-element.412, f32[4,8,128]{2,1,0:T(8,128)S(1)} %get-tuple-element.413, bf16[4,896,256]{2,1,0:T(8,128)(2,1)S(1)} %copy-done.4, bf16[4,128,8,128]{1,3,2,0:T(8,128)(2,1)S(1)} %copy.188, ...), kind=kOutput, calls=%fused_computation.11.clone.1 | convolution fusion | flops 958398464 | bytes 24019456 | tf_op jit(solution)/shard_map/while/body/eval_jaxpr/vmap(bpd,nd->pbn)/dot_general | solution.py:27
  474.2 9.5 %while.25 = (s32[]{:T(128)}, bf16[4864,256]{1,0:T(8,128)(2,1)}, s32[4,2]{0,1:T(2,128)S(1)}, bf16[4,896,256]{2,1,0:T(8,128)(2,1)S(1)}, s32[]{:T(128)}) while((s32[]{:T(128)}, bf16[4864,256]{1,0:T(8,128)(2,1)}, s32[4,2]{0,1:T(2,128)S(1)}, bf16[4,896,256]{2,1,0:T(8,128)(2,1)S(1)}, s32[]{:T(128)}) %tuple.86), condition=%wide.while_cond.1, body=%wide.while_body.1.sunk | while | flops 2 | bytes 917609 | solution.py:91
  483.8 10.0 %fusion.113 = (f32[4,8,128]{2,1,0:T(8,128)S(1)}, f32[4,8,128,896]{2,3,1,0:T(8,128)}) fusion(pred[4,128,896]{1,2,0:T(8,128)(4,1)S(1)} %broadcast_and_fusion.2, bf16[16,128,8,128]{1,3,2,0:T(8,128)(2,1)} %get-tuple-element.513, s32[]{:T(128)S(6)} %select_n.197, bf16[4,896,256]{2,1,0:T(8,128)(2,1)S(1)} %get-tuple-element.411), kind=kOutput, calls=%fused_computation.105.clone.1 | convolution fusion | flops 957875072 | bytes 17580036 | tf_op jit(solution)/shard_map/while/body/eval_jaxpr/vmap()/sub | solution.py:20
  493.8 9.9 %fusion.114 = bf16[4,8,128,896]{2,3,1,0:T(8,128)(2,1)} fusion(f32[4,8,128,896]{2,3,1,0:T(8,128)} %get-tuple-element.412, f32[4,8,128]{2,1,0:T(8,128)S(1)} %get-tuple-element.413), kind=kLoop, calls=%fused_computation.19.clone.1 | loop fusion | flops 7340032 | bytes 22036480 | tf_op jit(solution)/shard_map/while/body/eval_jaxpr/vmap()/convert_element_type | solution.py:22
  511.7 8.5 %fusion.115 = bf16[4,8,128,896]{2,3,1,0:T(8,128)(2,1)} fusion(f32[4,8,128]{2,1,0:T(8,128)S(1)} %bitcast.276, f32[4,8,128,896]{2,3,1,0:T(8,128)} %get-tuple-element.412, f32[4,8,128]{2,1,0:T(8,128)S(1)} %get-tuple-element.413, bf16[4,896,256]{2,1,0:T(8,128)(2,1)S(1)} %copy-done.4, bf16[4,128,8,128]{1,3,2,0:T(8,128)(2,1)S(1)} %copy.188, ...), kind=kOutput, calls=%fused_computation.11.clone.1 | convolution fusion | flops 958398464 | bytes 24019456 | tf_op jit(solution)/shard_map/while/body/eval_jaxpr/vmap(bpd,nd->pbn)/dot_general | solution.py:27
  545.5 36.1 %reduce-scatter.2.cloned.1.call-done = bf16[1024,256]{1,0:T(8,128)(2,1)} async-done(((bf16[4096,256]{1,0:T(8,128)(2,1)}), bf16[1024,256]{1,0:T(8,128)(2,1)}) %reduce-scatter.2.cloned.1.call-update) | async-done | bytes 524304 | tf_op jit(solution)/shard_map/reduce_scatter | solution.py:134
  585.1 19.8 %all-to-all-done.5 = bf16[4,4,128,1024]{2,3,1,0:T(8,128)(2,1)} async-done(((bf16[4,4,128,1024]{2,3,1,0:T(8,128)(2,1)}), bf16[4,4,128,1024]{2,3,1,0:T(8,128)(2,1)}, u32[]{:S(2)}, u32[]{:S(2)}) %all-to-all-start.5) | async-done | bytes 4194336 | tf_op jit(solution)/shard_map/all_to_all | solution.py:123
  608.5 6.3 copy.139
  636.5 23.8 %reshape.247 = bf16[2048,1,1024]{2,1,0:T(2,128)(2,1)} reshape(bf16[4,4,128,8,128]{4,3,2,1,0:T(8,128)(2,1)} %get-tuple-element.68) | data formatting | bytes 8388608 | tf_op jit(solution)/shard_map/reshape | solution.py:118
  660.4 26.0 %reduce.6 = bf16[2048,1024]{1,0:T(8,128)(2,1)} reduce(bf16[2048,1,1024]{2,1,0:T(2,128)(2,1)} %reshape.247, bf16[]{:T(256)} %broadcast.238), dimensions={1}, to_apply=%reshape.247.reduce_sub_computation | reduce | bytes 8388610 | tf_op jit(solution)/shard_map/reshape | solution.py:118
  686.4 7.8 reshape.256
  718.5 73.7 %all-to-all-done.4 = bf16[8,2,131072]{2,1,0:T(2,128)(2,1)} async-done(((bf16[8,2,131072]{2,1,0:T(2,128)(2,1)}), bf16[8,2,131072]{2,1,0:T(2,128)(2,1)}, u32[]{:S(2)}, u32[]{:S(2)}) %all-to-all-start.4) | async-done | bytes 4194336 | tf_op jit(solution)/shard_map/all_to_all | solution.py:119
  792.1 8.8 %reshape.257 = bf16[2048,1,1024]{2,1,0:T(2,128)(2,1)} reshape(bf16[8,2,131072]{2,1,0:T(2,128)(2,1)} %all-to-all-done.4) | data formatting | bytes 8388608
  800.9 7.1 copy.170
  808.0 6.5 copy.138
  (340 shorter events, 314.9 us)
Async XLA Ops:
  10.1 21.8 %all-to-all-start = ((bf16[128,8,256]{2,0,1:T(8,128)(2,1)}), bf16[128,8,256]{2,0,1:T(8,128)(2,1)S(1)}, u32[]{:S(2)}, u32[]{:S(2)}) async-start(bf16[128,8,256]{2,0,1:T(8,128)(2,1)} %maximum_bitcast_fusion), calls=%async_computation | async-start | bytes 1048576 | tf_op jit(solution)/shard_map/all_to_all | solution.py:60
  31.9 8.4 %copy-start.6 = (bf16[128,8,256]{2,0,1:T(8,128)(2,1)}, bf16[128,8,256]{2,0,1:T(8,128)(2,1)S(1)}, u32[]{:S(2)}) copy-start(bf16[128,8,256]{2,0,1:T(8,128)(2,1)S(1)} %all-to-all-done) | copy-start | bytes 1572868
  31.9 52.1 %all-to-all-start.1 = ((bf16[128,8,1024]{2,0,1:T(8,128)(2,1)}), bf16[128,8,1024]{2,0,1:T(8,128)(2,1)S(1)}, u32[]{:S(2)}, u32[]{:S(2)}) async-start(bf16[128,8,1024]{2,0,1:T(8,128)(2,1)} %copy.131), calls=%async_computation.1 | async-start | bytes 4194304 | tf_op jit(solution)/shard_map/all_to_all | solution.py:59
  83.9 4.7 copy-start.7
  83.9 97.2 %all-to-all-start.3 = ((bf16[256,8,1024]{2,0,1:T(8,128)(2,1)}), bf16[256,8,1024]{2,0,1:T(8,128)(2,1)}, u32[]{:S(2)}, u32[]{:S(2)}) async-start(bf16[256,8,1024]{2,0,1:T(8,128)(2,1)} %bitcast.255), calls=%async_computation.3 | async-start | bytes 8388608 | tf_op jit(solution)/shard_map/all_to_all | solution.py:64
  88.6 97.8 %all-gather.2.cloned.1.call-start = ((), (), s32[]{:S(2)}) async-start(), calls=%async_computation.9 | async-start | bytes 2621440 | tf_op jit(solution)/shard_map/all_gather | solution.py:62
  103.4 82.9 %copy-start.9 = (s32[32]{0:T(128)S(1)}, s32[32]{0:T(128)}, u32[]{:S(2)}) copy-start(s32[32]{0:T(128)} %param.12) | copy-start | bytes 388
  181.2 53.0 %all-to-all-start.2 = ((bf16[4,4,128,1024]{2,3,1,0:T(8,128)(2,1)}), bf16[4,4,128,1024]{2,3,1,0:T(8,128)(2,1)}, u32[]{:S(2)}, u32[]{:S(2)}) async-start(bf16[4,4,128,1024]{2,3,1,0:T(8,128)(2,1)} %broadcast_select_fusion.3), calls=%async_computation.2 | async-start | bytes 8388608 | tf_op jit(solution)/shard_map/all_to_all | solution.py:75
  186.0 395.6 %reduce-scatter.2.cloned.1.call-start = ((), (), s32[]{:S(2)}) async-start(), calls=%async_computation.10 | async-start | bytes 2621440 | tf_op jit(solution)/shard_map/reduce_scatter | solution.py:134
  259.8 19.9 %copy-start.3 = (bf16[4,896,256]{2,1,0:T(8,128)(2,1)}, bf16[4,896,256]{2,1,0:T(8,128)(2,1)S(1)}, u32[]{:S(2)}) copy-start(bf16[4,896,256]{2,1,0:T(8,128)(2,1)S(1)} %get-tuple-element.411) | copy-start | bytes 5505028 | tf_op jit(solution)/shard_map/while
  279.7 5.6 copy-start.1
  297.9 5.9 copy-start
  297.9 10.5 %slice-start = ((s8[4980736]{0:T(1024)(128)(4,1)}), s8[4194304]{0:T(1024)(128)(4,1)S(1)}, s32[]{:S(2)}) async-start(s8[4980736]{0:T(1024)(128)(4,1)} %bitcast.249), calls=%async_computation.11 | async-start | bytes 8388608 | tf_op jit(solution)/shard_map/while
  334.5 19.9 %copy-start.3 = (bf16[4,896,256]{2,1,0:T(8,128)(2,1)}, bf16[4,896,256]{2,1,0:T(8,128)(2,1)S(1)}, u32[]{:S(2)}) copy-start(bf16[4,896,256]{2,1,0:T(8,128)(2,1)S(1)} %get-tuple-element.411) | copy-start | bytes 5505028 | tf_op jit(solution)/shard_map/while
  354.3 5.6 copy-start.1
  372.6 5.9 copy-start
  372.6 10.5 %slice-start = ((s8[4980736]{0:T(1024)(128)(4,1)}), s8[4194304]{0:T(1024)(128)(4,1)S(1)}, s32[]{:S(2)}) async-start(s8[4980736]{0:T(1024)(128)(4,1)} %bitcast.249), calls=%async_computation.11 | async-start | bytes 8388608 | tf_op jit(solution)/shard_map/while
  378.5 4.7 slice-start.1
  409.1 19.9 %copy-start.3 = (bf16[4,896,256]{2,1,0:T(8,128)(2,1)}, bf16[4,896,256]{2,1,0:T(8,128)(2,1)S(1)}, u32[]{:S(2)}) copy-start(bf16[4,896,256]{2,1,0:T(8,128)(2,1)S(1)} %get-tuple-element.411) | copy-start | bytes 5505028 | tf_op jit(solution)/shard_map/while
  429.0 5.6 copy-start.1
  447.3 5.9 copy-start
  447.3 10.5 %slice-start = ((s8[4980736]{0:T(1024)(128)(4,1)}), s8[4194304]{0:T(1024)(128)(4,1)S(1)}, s32[]{:S(2)}) async-start(s8[4980736]{0:T(1024)(128)(4,1)} %bitcast.249), calls=%async_computation.11 | async-start | bytes 8388608 | tf_op jit(solution)/shard_map/while
  483.8 19.9 %copy-start.3 = (bf16[4,896,256]{2,1,0:T(8,128)(2,1)}, bf16[4,896,256]{2,1,0:T(8,128)(2,1)S(1)}, u32[]{:S(2)}) copy-start(bf16[4,896,256]{2,1,0:T(8,128)(2,1)S(1)} %get-tuple-element.411) | copy-start | bytes 5505028 | tf_op jit(solution)/shard_map/while
  503.7 5.6 copy-start.1
  521.9 5.9 copy-start
  521.9 10.5 %slice-start = ((s8[4980736]{0:T(1024)(128)(4,1)}), s8[4194304]{0:T(1024)(128)(4,1)S(1)}, s32[]{:S(2)}) async-start(s8[4980736]{0:T(1024)(128)(4,1)} %bitcast.249), calls=%async_computation.11 | async-start | bytes 8388608 | tf_op jit(solution)/shard_map/while
  540.6 64.3 %all-to-all-start.5 = ((bf16[4,4,128,1024]{2,3,1,0:T(8,128)(2,1)}), bf16[4,4,128,1024]{2,3,1,0:T(8,128)(2,1)}, u32[]{:S(2)}, u32[]{:S(2)}) async-start(bf16[4,4,128,1024]{2,3,1,0:T(8,128)(2,1)} %bitcast.264), calls=%async_computation.5 | async-start | bytes 8388608 | tf_op jit(solution)/shard_map/all_to_all | solution.py:123
  604.9 25.6 %all-to-all-start.7 = ((bf16[8,2,16384]{2,1,0:T(2,128)(2,1)}), bf16[8,2,16384]{2,1,0:T(2,128)(2,1)S(1)}, u32[]{:S(2)}, u32[]{:S(2)}) async-start(bf16[8,2,16384]{2,1,0:T(2,128)(2,1)} %reshape.260), calls=%async_computation.8 | async-start | bytes 1048576 | tf_op jit(solution)/shard_map/all_to_all | solution.py:138
  608.5 6.6 copy-start.8
  630.5 29.8 %copy-start.5 = (bf16[8,2,16384]{2,1,0:T(2,128)(2,1)}, bf16[8,2,16384]{2,1,0:T(2,128)(2,1)S(1)}, u32[]{:S(2)}) copy-start(bf16[8,2,16384]{2,1,0:T(2,128)(2,1)S(1)} %all-to-all-done.7) | copy-start | bytes 1572868
  630.5 63.6 %all-to-all-start.6 = ((bf16[8,2,65536]{2,1,0:T(2,128)(2,1)}), bf16[8,2,65536]{2,1,0:T(2,128)(2,1)S(1)}, u32[]{:S(2)}, u32[]{:S(2)}) async-start(bf16[8,2,65536]{2,1,0:T(2,128)(2,1)} %reshape.258), calls=%async_computation.6 | async-start | bytes 4194304 | tf_op jit(solution)/shard_map/all_to_all | solution.py:131
  694.2 97.9 %all-to-all-start.4 = ((bf16[8,2,131072]{2,1,0:T(2,128)(2,1)}), bf16[8,2,131072]{2,1,0:T(2,128)(2,1)}, u32[]{:S(2)}, u32[]{:S(2)}) async-start(bf16[8,2,131072]{2,1,0:T(2,128)(2,1)} %reshape.256), calls=%async_computation.4 | async-start | bytes 8388608 | tf_op jit(solution)/shard_map/all_to_all | solution.py:119
  (11 other events, 32.6 us)
Sparse Core Ops, SparseCore 0:
  91.0 23.8 all-gather.1
  540.7 40.8 reduce-scatter.1
where the time goes:
time: 833 us; the launch traced here: 828 us
  waiting for transfers between devices  299 us (36%)
  local copies, waits for them, and re-layouts  230 us (28%)
  matrix products  144 us (17%)
  other arithmetic  85.5 us (10%)
  starting transfers between devices  41 us (5%)
  between operations  14.3 us (2%)
  loops' own time  13.8 us (2%)
    all_to_all x1, waiting for transfers between devices, body(): lax.all_to_all(grad_split, 'head', split_axis=1, concat_axis=0, tiled=True)  77.7 us
    all_to_all x1, waiting for transfers between devices, body(): lax.all_to_all(out_slots, 'head', split_axis=0, concat_axis=1, tiled=True)  73.7 us
    unnamed x27, local copies, waits for them, and re-layouts  60.6 us
    gather x96, local copies, waits for them, and re-layouts  59.3 us
    all_to_all x1, waiting for transfers between devices, body(): lax.all_to_all(query_split, 'head', split_axis=1, concat_axis=0, tiled=True)  43.6 us
    sub x4, matrix products, slot_pass(): scores - rowmax  39.8 us
    convert_element_type x4, other arithmetic, slot_pass(): weights_b = weights.astype(jnp.bfloat16)  39.7 us
    all_to_all x1, waiting for transfers between devices, body(): lax.all_to_all(outgoing, 'seq', split_axis=0, concat_axis=0, tiled=True)  39.3 us
  transfers between devices with their start and end apart: 10, of which 7 were waited for; matrix products, arithmetic and copies ran while one was open for 16% of the time, Pallas kernels for 0%

commit v1 on v0

--- a/solution.py
+++ b/solution.py
@@ -9,6 +9,26 @@
 DH = 128
 BLOCK = 128
 DOCMAX = 7
+
+
+def remake_meshes(x_part, pos_dim, axis_no):
+    u1, e_now = (lax.axis_size("head"), lax.axis_index("head"))
+    p_next = x_part.shape[pos_dim] // u1
+    spare = list(x_part.shape)
+    spare[pos_dim] = p_next
+    piece_out = spare[axis_no]
+    spare[axis_no] = piece_out * u1
+    everything = jnp.zeros(spare, x_part.dtype)
+    t = 0
+    while t < u1:
+        e_next = lax.dynamic_slice_in_dim(x_part, (e_now ^ t) * p_next, p_next, axis=pos_dim)
+        if t:
+            e_next = lax.ppermute(e_next, "head", tuple(((dev, dev ^ t) for dev in range(u1))))
+        everything = lax.dynamic_update_slice_in_dim(
+            everything, e_next, (e_now ^ t) * piece_out, axis=axis_no
+        )
+        t += 1
+    return everything
 
 
 def slot_pass(queries, cotangent, keys_win, values_win, allowed, alive_flag, factor):
@@ -116,9 +136,7 @@
         group_step, partial_init, jnp.arange(group_count)
     )
     out_slots = outputs.reshape(slot_total * BLOCK, 1, per_dev * DH)
-    attn_out = lax.all_to_all(out_slots, "head", split_axis=0, concat_axis=1, tiled=True).reshape(
-        2 * tok_count, QH * DH
-    )
+    attn_out = remake_meshes(out_slots, 0, 1).reshape(2 * tok_count, QH * DH)
     back_slots = grad_rows.reshape(seq_count, slot_cap, BLOCK, per_dev * DH)
     returned = lax.all_to_all(back_slots, "seq", split_axis=0, concat_axis=0, tiled=True).reshape(
         slot_total, BLOCK, per_dev * DH

time: 833 us -> 860 us (1.032); the launches traced: 828 us -> 844 us
  starting transfers between devices: 41 us -> 53.4 us
  other arithmetic: 85.5 us -> 94.7 us
    ppermute x0 -> x7, waiting for transfers between devices: none -> 79 us  [remake_meshes(): lax.ppermute(e_next, 'head', tuple(((dev, dev ^ t) for dev in range(u1))))]
    all_to_all x1 -> x0, waiting for transfers between devices: 73.7 us -> none  [body(): lax.all_to_all(out_slots, 'head', split_axis=0, concat_axis=1, tiled=True)]
    dynamic_update_slice x16, other arithmetic: 2.86 us -> 38 us  [group_step(): lax.dynamic_update_slice_in_dim(partial_value, current + updates[member],...]
    dynamic_update_slice x0 -> x8, local copies, waits for them, and re-layouts: none -> 34.1 us  [remake_meshes(): lax.dynamic_update_slice_in_dim(everything, e_next, (e_now ^ t) * piece_o...]
    reshape x1 -> x0, other arithmetic: 26 us -> none  [body(): out_slots = outputs.reshape(slot_total * BLOCK, 1, per_dev * DH)]
    unnamed x27 -> x26, local copies, waits for them, and re-layouts: 60.6 us -> 40.2 us
    ppermute x0 -> x7, starting transfers between devices: none -> 18.4 us  [remake_meshes(): lax.ppermute(e_next, 'head', tuple(((dev, dev ^ t) for dev in range(u1))))]
    reshape x2 -> x1, local copies, waits for them, and re-layouts: 24.3 us -> 7.28 us  [body(): out_slots = outputs.reshape(slot_total * BLOCK, 1, per_dev * DH)]
  transfers between devices with their start and end apart: 10 -> 16, of which waited for: 7 -> 11; matrix products, arithmetic and copies ran while one was open for 16% -> 14% of each run, Pallas kernels for 0% -> 0%
where the time goes in v1:
time: 860 us; the launch traced here: 844 us
  waiting for transfers between devices  304 us (35%)
  local copies, waits for them, and re-layouts  225 us (26%)
  matrix products  139 us (16%)
  other arithmetic  94.7 us (11%)
  starting transfers between devices  53.4 us (6%)
  between operations  14.3 us (2%)
  loops' own time  13.5 us (2%)
    ppermute x7, waiting for transfers between devices, remake_meshes(): lax.ppermute(e_next, 'head', tuple(((dev, dev ^ t) for dev in range(u1))))  79 us
    all_to_all x1, waiting for transfers between devices, body(): lax.all_to_all(grad_split, 'head', split_axis=1, concat_axis=0, tiled=True)  77.7 us
    gather x96, local copies, waits for them, and re-layouts  59.6 us
    all_to_all x1, waiting for transfers between devices, body(): lax.all_to_all(query_split, 'head', split_axis=1, concat_axis=0, tiled=True)  43.6 us
    unnamed x26, local copies, waits for them, and re-layouts  40.2 us
    sub x4, matrix products, slot_pass(): scores - rowmax  40 us
    convert_element_type x4, other arithmetic, slot_pass(): weights_b = weights.astype(jnp.bfloat16)  39.8 us
    all_to_all x1, waiting for transfers between devices, body(): lax.all_to_all(outgoing, 'seq', split_axis=0, concat_axis=0, tiled=True)  39.3 us
  transfers between devices with their start and end apart: 16, of which 11 were waited for; matrix products, arithmetic and copies ran while one was open for 14% of the time, Pallas kernels for 0%

profile of v1, /device:TPU:0, one launch (start us, length us, event | category | flops | bytes accessed | tf_op | source)
XLA Modules:
  0.0 844.1 jit_solution(11111543176440085091)
XLA Ops:
  10.1 7.3 all-to-all-start
  23.2 8.7 %all-to-all-done = bf16[128,8,256]{2,0,1:T(8,128)(2,1)S(1)} async-done(((bf16[128,8,256]{2,0,1:T(8,128)(2,1)}), bf16[128,8,256]{2,0,1:T(8,128)(2,1)S(1)}, u32[]{:S(2)}, u32[]{:S(2)}) %all-to-all-start) | async-done | bytes 524320 | tf_op jit(solution)/shard_map/all_to_all | solution.py:80
  40.3 43.6 %all-to-all-done.1 = bf16[128,8,1024]{2,0,1:T(8,128)(2,1)S(1)} async-done(((bf16[128,8,1024]{2,0,1:T(8,128)(2,1)}), bf16[128,8,1024]{2,0,1:T(8,128)(2,1)S(1)}, u32[]{:S(2)}, u32[]{:S(2)}) %all-to-all-start.1) | async-done | bytes 2097184 | tf_op jit(solution)/shard_map/all_to_all | solution.py:79
  103.5 77.7 %all-to-all-done.3 = bf16[256,8,1024]{2,0,1:T(8,128)(2,1)} async-done(((bf16[256,8,1024]{2,0,1:T(8,128)(2,1)}), bf16[256,8,1024]{2,0,1:T(8,128)(2,1)}, u32[]{:S(2)}, u32[]{:S(2)}) %all-to-all-start.3) | async-done | bytes 4194336 | tf_op jit(solution)/shard_map/all_to_all | solution.py:84
  194.9 39.3 %all-to-all-done.2 = bf16[4,4,128,1024]{2,3,1,0:T(8,128)(2,1)} async-done(((bf16[4,4,128,1024]{2,3,1,0:T(8,128)(2,1)}), bf16[4,4,128,1024]{2,3,1,0:T(8,128)(2,1)}, u32[]{:S(2)}, u32[]{:S(2)}) %all-to-all-start.2) | async-done | bytes 4194336 | tf_op jit(solution)/shard_map/all_to_all | solution.py:95
  236.8 327.1 %while.23 = (s32[]{:T(128)}, f32[4864,256]{0,1:T(8,128)}, bf16[4,4,128,8,128]{4,3,2,1,0:T(8,128)(2,1)}, bf16[4,4,128,8,128]{2,4,3,1,0:T(8,128)(2,1)}, s32[4]{0:T...) while((s32[]{:T(128)}, f32[4864,256]{0,1:T(8,128)}, ...), condition=%wide.region_4.5_spmd.clone, body=%wide.region_0.0_spmd.clone.sunk | while | flops 5688947712 | bytes 213390656 | solution.py:135
  248.4 9.6 %while.25 = (s32[]{:T(128)}, bf16[4864,256]{1,0:T(8,128)(2,1)}, s32[4,2]{0,1:T(2,128)S(1)}, bf16[4,896,256]{2,1,0:T(8,128)(2,1)S(1)}, s32[]{:T(128)}) while((s32[]{:T(128)}, bf16[4864,256]{1,0:T(8,128)(2,1)}, s32[4,2]{0,1:T(2,128)S(1)}, bf16[4,896,256]{2,1,0:T(8,128)(2,1)S(1)}, s32[]{:T(128)}) %tuple.93), condition=%wide.while_cond.1, body=%wide.while_body.1.sunk | while | flops 2 | bytes 917609 | solution.py:111
  258.0 10.0 %fusion.114 = (f32[4,8,128]{2,1,0:T(8,128)S(1)}, f32[4,8,128,896]{2,3,1,0:T(8,128)}) fusion(pred[4,128,896]{1,2,0:T(8,128)(4,1)S(1)} %broadcast_and_fusion.2, bf16[16,128,8,128]{1,3,2,0:T(8,128)(2,1)} %get-tuple-element.521, s32[]{:T(128)S(6)} %select_n.261, bf16[4,896,256]{2,1,0:T(8,128)(2,1)S(1)} %get-tuple-element.419), kind=kOutput, calls=%fused_computation.120.clone.1 | convolution fusion | flops 957875072 | bytes 17580036 | tf_op jit(solution)/shard_map/while/body/eval_jaxpr/vmap()/sub | solution.py:40
  268.0 9.9 %fusion.115 = bf16[4,8,128,896]{2,3,1,0:T(8,128)(2,1)} fusion(f32[4,8,128,896]{2,3,1,0:T(8,128)} %get-tuple-element.420, f32[4,8,128]{2,1,0:T(8,128)S(1)} %get-tuple-element.421), kind=kLoop, calls=%fused_computation.19.clone.1 | loop fusion | flops 7340032 | bytes 22036480 | tf_op jit(solution)/shard_map/while/body/eval_jaxpr/vmap()/convert_element_type | solution.py:42
  283.4 6.7 fusion.116
  330.1 9.6 %while.25 = (s32[]{:T(128)}, bf16[4864,256]{1,0:T(8,128)(2,1)}, s32[4,2]{0,1:T(2,128)S(1)}, bf16[4,896,256]{2,1,0:T(8,128)(2,1)S(1)}, s32[]{:T(128)}) while((s32[]{:T(128)}, bf16[4864,256]{1,0:T(8,128)(2,1)}, s32[4,2]{0,1:T(2,128)S(1)}, bf16[4,896,256]{2,1,0:T(8,128)(2,1)S(1)}, s32[]{:T(128)}) %tuple.93), condition=%wide.while_cond.1, body=%wide.while_body.1.sunk | while | flops 2 | bytes 917609 | solution.py:111
  339.7 10.0 %fusion.114 = (f32[4,8,128]{2,1,0:T(8,128)S(1)}, f32[4,8,128,896]{2,3,1,0:T(8,128)}) fusion(pred[4,128,896]{1,2,0:T(8,128)(4,1)S(1)} %broadcast_and_fusion.2, bf16[16,128,8,128]{1,3,2,0:T(8,128)(2,1)} %get-tuple-element.521, s32[]{:T(128)S(6)} %select_n.261, bf16[4,896,256]{2,1,0:T(8,128)(2,1)S(1)} %get-tuple-element.419), kind=kOutput, calls=%fused_computation.120.clone.1 | convolution fusion | flops 957875072 | bytes 17580036 | tf_op jit(solution)/shard_map/while/body/eval_jaxpr/vmap()/sub | solution.py:40
  349.7 9.9 %fusion.115 = bf16[4,8,128,896]{2,3,1,0:T(8,128)(2,1)} fusion(f32[4,8,128,896]{2,3,1,0:T(8,128)} %get-tuple-element.420, f32[4,8,128]{2,1,0:T(8,128)S(1)} %get-tuple-element.421), kind=kLoop, calls=%fused_computation.19.clone.1 | loop fusion | flops 7340032 | bytes 22036480 | tf_op jit(solution)/shard_map/while/body/eval_jaxpr/vmap()/convert_element_type | solution.py:42
  365.1 6.7 fusion.116
  411.9 9.6 %while.25 = (s32[]{:T(128)}, bf16[4864,256]{1,0:T(8,128)(2,1)}, s32[4,2]{0,1:T(2,128)S(1)}, bf16[4,896,256]{2,1,0:T(8,128)(2,1)S(1)}, s32[]{:T(128)}) while((s32[]{:T(128)}, bf16[4864,256]{1,0:T(8,128)(2,1)}, s32[4,2]{0,1:T(2,128)S(1)}, bf16[4,896,256]{2,1,0:T(8,128)(2,1)S(1)}, s32[]{:T(128)}) %tuple.93), condition=%wide.while_cond.1, body=%wide.while_body.1.sunk | while | flops 2 | bytes 917609 | solution.py:111
  421.5 10.0 %fusion.114 = (f32[4,8,128]{2,1,0:T(8,128)S(1)}, f32[4,8,128,896]{2,3,1,0:T(8,128)}) fusion(pred[4,128,896]{1,2,0:T(8,128)(4,1)S(1)} %broadcast_and_fusion.2, bf16[16,128,8,128]{1,3,2,0:T(8,128)(2,1)} %get-tuple-element.521, s32[]{:T(128)S(6)} %select_n.261, bf16[4,896,256]{2,1,0:T(8,128)(2,1)S(1)} %get-tuple-element.419), kind=kOutput, calls=%fused_computation.120.clone.1 | convolution fusion | flops 957875072 | bytes 17580036 | tf_op jit(solution)/shard_map/while/body/eval_jaxpr/vmap()/sub | solution.py:40
  431.5 9.9 %fusion.115 = bf16[4,8,128,896]{2,3,1,0:T(8,128)(2,1)} fusion(f32[4,8,128,896]{2,3,1,0:T(8,128)} %get-tuple-element.420, f32[4,8,128]{2,1,0:T(8,128)S(1)} %get-tuple-element.421), kind=kLoop, calls=%fused_computation.19.clone.1 | loop fusion | flops 7340032 | bytes 22036480 | tf_op jit(solution)/shard_map/while/body/eval_jaxpr/vmap()/convert_element_type | solution.py:42
  446.9 6.7 fusion.116
  493.7 9.6 %while.25 = (s32[]{:T(128)}, bf16[4864,256]{1,0:T(8,128)(2,1)}, s32[4,2]{0,1:T(2,128)S(1)}, bf16[4,896,256]{2,1,0:T(8,128)(2,1)S(1)}, s32[]{:T(128)}) while((s32[]{:T(128)}, bf16[4864,256]{1,0:T(8,128)(2,1)}, s32[4,2]{0,1:T(2,128)S(1)}, bf16[4,896,256]{2,1,0:T(8,128)(2,1)S(1)}, s32[]{:T(128)}) %tuple.93), condition=%wide.while_cond.1, body=%wide.while_body.1.sunk | while | flops 2 | bytes 917609 | solution.py:111
  503.3 10.0 %fusion.114 = (f32[4,8,128]{2,1,0:T(8,128)S(1)}, f32[4,8,128,896]{2,3,1,0:T(8,128)}) fusion(pred[4,128,896]{1,2,0:T(8,128)(4,1)S(1)} %broadcast_and_fusion.2, bf16[16,128,8,128]{1,3,2,0:T(8,128)(2,1)} %get-tuple-element.521, s32[]{:T(128)S(6)} %select_n.261, bf16[4,896,256]{2,1,0:T(8,128)(2,1)S(1)} %get-tuple-element.419), kind=kOutput, calls=%fused_computation.120.clone.1 | convolution fusion | flops 957875072 | bytes 17580036 | tf_op jit(solution)/shard_map/while/body/eval_jaxpr/vmap()/sub | solution.py:40
  513.3 9.9 %fusion.115 = bf16[4,8,128,896]{2,3,1,0:T(8,128)(2,1)} fusion(f32[4,8,128,896]{2,3,1,0:T(8,128)} %get-tuple-element.420, f32[4,8,128]{2,1,0:T(8,128)S(1)} %get-tuple-element.421), kind=kLoop, calls=%fused_computation.19.clone.1 | loop fusion | flops 7340032 | bytes 22036480 | tf_op jit(solution)/shard_map/while/body/eval_jaxpr/vmap()/convert_element_type | solution.py:42
  528.7 6.7 fusion.116
  574.0 36.1 %reduce-scatter.2.cloned.1.call-done = bf16[1024,256]{1,0:T(8,128)(2,1)} async-done(((bf16[4096,256]{1,0:T(8,128)(2,1)}), bf16[1024,256]{1,0:T(8,128)(2,1)}) %reduce-scatter.2.cloned.1.call-update) | async-done | bytes 524304 | tf_op jit(solution)/shard_map/reduce_scatter | solution.py:152
  613.6 19.8 %all-to-all-done.4 = bf16[4,4,128,1024]{2,3,1,0:T(8,128)(2,1)} async-done(((bf16[4,4,128,1024]{2,3,1,0:T(8,128)(2,1)}), bf16[4,4,128,1024]{2,3,1,0:T(8,128)(2,1)}, u32[]{:S(2)}, u32[]{:S(2)}) %all-to-all-start.4) | async-done | bytes 4194336 | tf_op jit(solution)/shard_map/all_to_all | solution.py:141
  665.0 7.3 reshape.181
  685.9 16.0 %collective-permute-done = bf16[256,1,1024]{2,0,1:T(8,128)(2,1)} collective-permute-done((bf16[256,1,1024]{2,0,1:T(8,128)(2,1)}, bf16[256,1,1024]{2,0,1:T(8,128)(2,1)}, u32[]{:S(2)}, u32[]{:S(2)}) %collective-permute-start) | collective-permute-done | bytes 524320 | tf_op jit(solution)/shard_map/ppermute | solution.py:26
  701.9 7.3 collective-permute-start.5
  711.0 13.9 %collective-permute-done.1 = bf16[256,1,1024]{2,0,1:T(8,128)(2,1)} collective-permute-done((bf16[256,1,1024]{2,0,1:T(8,128)(2,1)}, bf16[256,1,1024]{2,0,1:T(8,128)(2,1)}, u32[]{:S(2)}, u32[]{:S(2)}) %collective-permute-start.1) | collective-permute-done | bytes 524320 | tf_op jit(solution)/shard_map/ppermute | solution.py:26
  738.0 32.9 %collective-permute-done.3 = bf16[256,1,1024]{2,0,1:T(8,128)(2,1)S(1)} collective-permute-done((bf16[256,1,1024]{2,0,1:T(8,128)(2,1)}, bf16[256,1,1024]{2,0,1:T(8,128)(2,1)S(1)}, u32[]{:S(2)}, u32[]{:S(2)}) %collective-permute-start.3) | collective-permute-done | bytes 524320 | tf_op jit(solution)/shard_map/ppermute | solution.py:26
  771.7 10.2 %collective-permute-done.4 = bf16[256,1,1024]{2,0,1:T(8,128)(2,1)S(1)} collective-permute-done((bf16[256,1,1024]{2,0,1:T(8,128)(2,1)}, bf16[256,1,1024]{2,0,1:T(8,128)(2,1)S(1)}, u32[]{:S(2)}, u32[]{:S(2)}) %collective-permute-start.4) | collective-permute-done | bytes 524320 | tf_op jit(solution)/shard_map/ppermute | solution.py:26
  790.7 19.6 %dynamic_update_slice.50 = bf16[256,8,1024]{2,1,0:T(8,128)(2,1)} dynamic-update-slice(bf16[256,8,1024]{2,1,0:T(8,128)(2,1)} %copy.137, bf16[256,1,1024]{2,1,0:T(2,128)(2,1)S(1)} %copy.138, s32[]{:T(128)} %constant.47.clone.1, s32[]{:T(128)S(6)} %select_n.185, s32[]{:T(128)} %constant.47.clone.1) | dynamic-update-slice | bytes 1048580 | tf_op jit(solution)/shard_map/dynamic_update_slice | solution.py:27
  810.4 8.5 %copy.177 = bf16[32,8,8,1024]{3,1,2,0:T(8,128)(2,1)} copy(bf16[32,8,8,1024]{3,2,1,0:T(8,128)(2,1)} %bitcast.250) | data formatting | bytes 8388608
  (340 shorter events, 383.4 us)
Async XLA Ops:
  10.1 21.8 %all-to-all-start = ((bf16[128,8,256]{2,0,1:T(8,128)(2,1)}), bf16[128,8,256]{2,0,1:T(8,128)(2,1)S(1)}, u32[]{:S(2)}, u32[]{:S(2)}) async-start(bf16[128,8,256]{2,0,1:T(8,128)(2,1)} %maximum_bitcast_fusion), calls=%async_computation | async-start | bytes 1048576 | tf_op jit(solution)/shard_map/all_to_all | solution.py:80
  31.9 8.5 %copy-start.7 = (bf16[128,8,256]{2,0,1:T(8,128)(2,1)}, bf16[128,8,256]{2,0,1:T(8,128)(2,1)S(1)}, u32[]{:S(2)}) copy-start(bf16[128,8,256]{2,0,1:T(8,128)(2,1)S(1)} %all-to-all-done) | copy-start | bytes 1572868
  31.9 52.1 %all-to-all-start.1 = ((bf16[128,8,1024]{2,0,1:T(8,128)(2,1)}), bf16[128,8,1024]{2,0,1:T(8,128)(2,1)S(1)}, u32[]{:S(2)}, u32[]{:S(2)}) async-start(bf16[128,8,1024]{2,0,1:T(8,128)(2,1)} %copy.131), calls=%async_computation.1 | async-start | bytes 4194304 | tf_op jit(solution)/shard_map/all_to_all | solution.py:79
  83.9 97.2 %all-to-all-start.3 = ((bf16[256,8,1024]{2,0,1:T(8,128)(2,1)}), bf16[256,8,1024]{2,0,1:T(8,128)(2,1)}, u32[]{:S(2)}, u32[]{:S(2)}) async-start(bf16[256,8,1024]{2,0,1:T(8,128)(2,1)} %bitcast.249), calls=%async_computation.3 | async-start | bytes 8388608 | tf_op jit(solution)/shard_map/all_to_all | solution.py:84
  88.6 97.8 %all-gather.2.cloned.1.call-start = ((), (), s32[]{:S(2)}) async-start(), calls=%async_computation.8 | async-start | bytes 2621440 | tf_op jit(solution)/shard_map/all_gather | solution.py:82
  103.5 82.8 %copy-start.10 = (s32[32]{0:T(128)S(1)}, s32[32]{0:T(128)}, u32[]{:S(2)}) copy-start(s32[32]{0:T(128)} %param.12) | copy-start | bytes 388
  181.2 53.1 %all-to-all-start.2 = ((bf16[4,4,128,1024]{2,3,1,0:T(8,128)(2,1)}), bf16[4,4,128,1024]{2,3,1,0:T(8,128)(2,1)}, u32[]{:S(2)}, u32[]{:S(2)}) async-start(bf16[4,4,128,1024]{2,3,1,0:T(8,128)(2,1)} %broadcast_select_fusion.3), calls=%async_computation.2 | async-start | bytes 8388608 | tf_op jit(solution)/shard_map/all_to_all | solution.py:95
  186.0 424.0 %reduce-scatter.2.cloned.1.call-start = ((), (), s32[]{:S(2)}) async-start(), calls=%async_computation.9 | async-start | bytes 2621440 | tf_op jit(solution)/shard_map/reduce_scatter | solution.py:152
  258.0 25.4 %copy-start.5 = (bf16[4,896,256]{2,1,0:T(8,128)(2,1)}, bf16[4,896,256]{2,1,0:T(8,128)(2,1)S(1)}, u32[]{:S(2)}) copy-start(bf16[4,896,256]{2,1,0:T(8,128)(2,1)S(1)} %get-tuple-element.419) | copy-start | bytes 5505028 | tf_op jit(solution)/shard_map/while
  290.1 6.0 copy-start.2
  305.5 5.6 copy-start.3
  339.7 25.4 %copy-start.5 = (bf16[4,896,256]{2,1,0:T(8,128)(2,1)}, bf16[4,896,256]{2,1,0:T(8,128)(2,1)S(1)}, u32[]{:S(2)}) copy-start(bf16[4,896,256]{2,1,0:T(8,128)(2,1)S(1)} %get-tuple-element.419) | copy-start | bytes 5505028 | tf_op jit(solution)/shard_map/while
  371.8 6.0 copy-start.2
  387.2 5.6 copy-start.3
  421.5 25.4 %copy-start.5 = (bf16[4,896,256]{2,1,0:T(8,128)(2,1)}, bf16[4,896,256]{2,1,0:T(8,128)(2,1)S(1)}, u32[]{:S(2)}) copy-start(bf16[4,896,256]{2,1,0:T(8,128)(2,1)S(1)} %get-tuple-element.419) | copy-start | bytes 5505028 | tf_op jit(solution)/shard_map/while
  453.6 6.0 copy-start.2
  469.1 5.6 copy-start.3
  503.3 25.4 %copy-start.5 = (bf16[4,896,256]{2,1,0:T(8,128)(2,1)}, bf16[4,896,256]{2,1,0:T(8,128)(2,1)S(1)}, u32[]{:S(2)}) copy-start(bf16[4,896,256]{2,1,0:T(8,128)(2,1)S(1)} %get-tuple-element.419) | copy-start | bytes 5505028 | tf_op jit(solution)/shard_map/while
  535.4 6.0 copy-start.2
  550.9 5.6 copy-start.3
  569.1 64.3 %all-to-all-start.4 = ((bf16[4,4,128,1024]{2,3,1,0:T(8,128)(2,1)}), bf16[4,4,128,1024]{2,3,1,0:T(8,128)(2,1)}, u32[]{:S(2)}, u32[]{:S(2)}) async-start(bf16[4,4,128,1024]{2,3,1,0:T(8,128)(2,1)} %bitcast.258), calls=%async_computation.4 | async-start | bytes 8388608 | tf_op jit(solution)/shard_map/all_to_all | solution.py:141
  633.4 25.6 %all-to-all-start.6 = ((bf16[8,2,16384]{2,1,0:T(2,128)(2,1)}), bf16[8,2,16384]{2,1,0:T(2,128)(2,1)S(1)}, u32[]{:S(2)}, u32[]{:S(2)}) async-start(bf16[8,2,16384]{2,1,0:T(2,128)(2,1)} %reshape.256), calls=%async_computation.7 | async-start | bytes 1048576 | tf_op jit(solution)/shard_map/all_to_all | solution.py:156
  637.0 6.6 copy-start.9
  659.0 13.3 %copy-start.6 = (bf16[8,2,16384]{2,1,0:T(2,128)(2,1)}, bf16[8,2,16384]{2,1,0:T(2,128)(2,1)S(1)}, u32[]{:S(2)}) copy-start(bf16[8,2,16384]{2,1,0:T(2,128)(2,1)S(1)} %all-to-all-done.6) | copy-start | bytes 1572868
  659.0 164.4 %all-to-all-start.5 = ((bf16[8,2,65536]{2,1,0:T(2,128)(2,1)}), bf16[8,2,65536]{2,1,0:T(2,128)(2,1)S(1)}, u32[]{:S(2)}, u32[]{:S(2)}) async-start(bf16[8,2,65536]{2,1,0:T(2,128)(2,1)} %reshape.254), calls=%async_computation.5 | async-start | bytes 4194304 | tf_op jit(solution)/shard_map/all_to_all | solution.py:149
  678.0 23.8 %collective-permute-start = (bf16[256,1,1024]{2,0,1:T(8,128)(2,1)}, bf16[256,1,1024]{2,0,1:T(8,128)(2,1)}, u32[]{:S(2)}, u32[]{:S(2)}) collective-permute-start(bf16[256,1,1024]{2,0,1:T(8,128)(2,1)} %get-tuple-element.260), channel_id=1, source_target_pairs={{0,1},{1,0},{2,3},{3,2},{4,5},{5,4},{6,7},{7,6},{8,9},{9,8},{10,11... | collective-permute-start | bytes 1572872 | tf_op jit(solution)/shard_map/ppermute | solution.py:26
  680.1 44.8 %collective-permute-start.1 = (bf16[256,1,1024]{2,0,1:T(8,128)(2,1)}, bf16[256,1,1024]{2,0,1:T(8,128)(2,1)}, u32[]{:S(2)}, u32[]{:S(2)}) collective-permute-start(bf16[256,1,1024]{2,0,1:T(8,128)(2,1)} %get-tuple-element.259), channel_id=1, source_target_pairs={{0,2},{1,3},{2,0},{3,1},{4,6},{5,7},{6,4},{7,5},{8,10},{9,11},{10,... | collective-permute-start | bytes 1572872 | tf_op jit(solution)/shard_map/ppermute | solution.py:26
  681.5 54.6 %collective-permute-start.2 = (bf16[256,1,1024]{2,0,1:T(8,128)(2,1)}, bf16[256,1,1024]{2,0,1:T(8,128)(2,1)}, u32[]{:S(2)}, u32[]{:S(2)}) collective-permute-start(bf16[256,1,1024]{2,0,1:T(8,128)(2,1)} %get-tuple-element.258), channel_id=1, source_target_pairs={{0,3},{1,2},{2,1},{3,0},{4,7},{5,6},{6,5},{7,4},{8,11},{9,10},{10,... | collective-permute-start | bytes 1572872 | tf_op jit(solution)/shard_map/ppermute | solution.py:26
  681.5 89.3 %collective-permute-start.3 = (bf16[256,1,1024]{2,0,1:T(8,128)(2,1)}, bf16[256,1,1024]{2,0,1:T(8,128)(2,1)S(1)}, u32[]{:S(2)}, u32[]{:S(2)}) collective-permute-start(bf16[256,1,1024]{2,0,1:T(8,128)(2,1)} %get-tuple-element.257), channel_id=1, source_target_pairs={{0,4},{1,5},{2,6},{3,7},{4,0},{5,1},{6,2},{7,3},{8,12},{9,13},{10,... | collective-permute-start | bytes 1572872 | tf_op jit(solution)/shard_map/ppermute | solution.py:26
  684.5 97.4 %collective-permute-start.4 = (bf16[256,1,1024]{2,0,1:T(8,128)(2,1)}, bf16[256,1,1024]{2,0,1:T(8,128)(2,1)S(1)}, u32[]{:S(2)}, u32[]{:S(2)}) collective-permute-start(bf16[256,1,1024]{2,0,1:T(8,128)(2,1)} %get-tuple-element.256), channel_id=1, source_target_pairs={{0,5},{1,4},{2,7},{3,6},{4,1},{5,0},{6,3},{7,2},{8,13},{9,12},{10,... | collective-permute-start | bytes 1572872 | tf_op jit(solution)/shard_map/ppermute | solution.py:26
  701.9 80.8 %collective-permute-start.5 = (bf16[256,1,1024]{2,0,1:T(8,128)(2,1)}, bf16[256,1,1024]{2,0,1:T(8,128)(2,1)S(1)}, u32[]{:S(2)}, u32[]{:S(2)}) collective-permute-start(bf16[256,1,1024]{2,0,1:T(8,128)(2,1)} %get-tuple-element.255), channel_id=1, source_target_pairs={{0,6},{1,7},{2,4},{3,5},{4,2},{5,3},{6,0},{7,1},{8,14},{9,15},{10,... | collective-permute-start | bytes 1572872 | tf_op jit(solution)/shard_map/ppermute | solution.py:26
  724.9 65.0 %collective-permute-start.6 = (bf16[256,1,1024]{2,0,1:T(8,128)(2,1)}, bf16[256,1,1024]{2,0,1:T(8,128)(2,1)S(1)}, u32[]{:S(2)}, u32[]{:S(2)}) collective-permute-start(bf16[256,1,1024]{2,0,1:T(8,128)(2,1)} %get-tuple-element.254), channel_id=1, source_target_pairs={{0,7},{1,6},{2,5},{3,4},{4,3},{5,2},{6,1},{7,0},{8,15},{9,14},{10,... | collective-permute-start | bytes 1572872 | tf_op jit(solution)/shard_map/ppermute | solution.py:26
  (10 other events, 31.7 us)
Sparse Core Ops, SparseCore 0:
  91.0 23.8 all-gather.1
  569.2 40.8 reduce-scatter.1
